TPU v7x, 32 devices: a whole 2x2x4 slice. The times are simulated.
32 devices in a mesh: subtree: 8 (over z, core), front: 4 (over y, x).
Axes of the slice: x: 2, y: 2, z: 4, core: 2. Of those that a mesh axis runs over, the one named last changes fastest.
Arguments:
- leaf_rhs: float32 [8, 2048, 256], P('subtree', 'front'), may hold values from -6 to 6
- mid_rhs: float32 [2, 4096, 256], P(None, 'front'), may hold values from -6 to 6
- root_rhs: float32 [10240, 256], P('front'), may hold values from -6 to 6
- leaf_lower: float32 [8, 2048, 2048], P('subtree', None, 'front'), may hold values from -0.125 to 0.125
- leaf_below: float32 [8, 2048, 2048], P('subtree', None, 'front'), may hold values from -0.125 to 0.125
- leaf_right: float32 [8, 2048, 2048], P('subtree', None, 'front'), may hold values from -0.125 to 0.125
- leaf_upper: float32 [8, 2048, 2048], P('subtree', None, 'front'), may hold values from -0.125 to 0.125
- mid_lower: float32 [2, 4096, 4096], P(None, 'subtree', 'front'), may hold values from -0.09375 to 0.09375
- mid_below: float32 [2, 4096, 4096], P(None, 'front', 'subtree'), may hold values from -0.09375 to 0.09375
- mid_right: float32 [2, 4096, 4096], P(None, 'subtree', 'front'), may hold values from -0.09375 to 0.09375
- mid_upper: float32 [2, 4096, 4096], P(None, 'front', 'subtree'), may hold values from -0.09375 to 0.09375
- root_lower: float32 [10240, 10240], P('subtree', 'front'), may hold values from -0.0625 to 0.0625
- root_upper: float32 [10240, 10240], P('front', 'subtree'), may hold values from -0.0625 to 0.0625
- leaf_parent: int32 [8], replicated, may hold values from 0 to 1, as said below
- leaf_sizes: int32 [8], replicated, may hold values from 1024 to 2048, as said below
- leaf_map: int32 [8, 16], replicated, may hold values from 0 to 63, as said below
- mid_map: int32 [2, 32], replicated, may hold values from 0 to 79, as said below
Outputs:
- leaf_sol: float32 [8, 2048, 256], P('subtree', 'front')
- mid_sol: float32 [2, 4096, 256], P(None, 'front')
- root_sol: float32 [10240, 256], P('front')
Inputs may be any that keep to these rules, and one draw needn't show every extreme that they name: `leaf_parent`: every level-1 front is the parent of at least one lowest-level front. `leaf_sizes`: a multiple of 128; some front has all 2048 rows live. `leaf_map`: a front's blocks go to distinct parent blocks; update block b of a lowest-level front, with c = b // 4, goes to c * 8 + i or to that plus 4096 / 128, for some i with 0 <= i < 8. `mid_map`: a front's blocks go to distinct root blocks; update block b of a level-1 front, with c = b // 8, goes to c * 20 + i for some i with 0 <= i < 20.
All inputs are finite; a program needn't handle non-finite values.
Results may differ from a plain program's by a relative error of at most 0.00013.
Values sent between devices are 32-bit elements; how exact they have to be, the bound alone decides.
No kernel may reach another device: no remote copies, remote signals or barrier semaphores. Data moves between devices by JAX's collectives and lax.ppermute only.
A program may use at most 128 MiB of HBM per device.

v0:
```python
import jax
import jax.numpy as jnp
from jax import lax
from jax.sharding import PartitionSpec as P

MID_PIV = 4096
BLOCK = 128


def leaf_product(matrix, vector):
    return lax.psum_scatter(
        jnp.dot(
            matrix, vector, preferred_element_type=jnp.float32, precision=lax.Precision.HIGHEST
        ),
        "front",
        scatter_dimension=0,
        tiled=True,
    )


def across_front(partial_value):
    return lax.psum(partial_value, "front")


def across_subtree(partial_value):
    return lax.psum(partial_value, "subtree")


def batched(matrix, vector):
    return jnp.einsum(
        "fab,fbr->far",
        matrix,
        vector,
        preferred_element_type=jnp.float32,
        precision=lax.Precision.HIGHEST,
    )


def leaf_select(parents, blocks, fronts, column, width):
    front_ids = jnp.arange(fronts, dtype=jnp.int32)[:, None, None, None, None]
    halves = jnp.arange(2, dtype=jnp.int32)[None, :, None, None, None]
    slots = jnp.arange(width, dtype=jnp.int32)[None, None, :, None, None]
    target = halves * (MID_PIV // BLOCK) + column * width + slots
    match_parent = parents[None, None, None, :, None] == front_ids
    match_block = blocks[None, None, None, :, :] == target
    return (match_parent & match_block).astype(jnp.float32)


def on_device(
    leaf_rhs,
    mid_rhs,
    root_rhs,
    leaf_lower,
    leaf_below,
    leaf_right,
    leaf_upper,
    mid_lower,
    mid_below,
    mid_right,
    mid_upper,
    root_lower,
    root_upper,
    leaf_parent,
    leaf_sizes,
    leaf_map,
    mid_map,
):
    group = lax.axis_index("subtree")
    column = lax.axis_index("front")
    local_rows = leaf_rhs.shape[1]
    scenarios = leaf_rhs.shape[2]
    leaf_width = local_rows // BLOCK
    fronts = mid_rhs.shape[0]
    mid_width = mid_rhs.shape[1] // BLOCK
    root_width = root_rhs.shape[0] // BLOCK
    own_size = lax.dynamic_slice_in_dim(leaf_sizes, group, 1)
    positions = column * local_rows + jnp.arange(local_rows, dtype=jnp.int32)
    live = (positions < own_size[0]).astype(jnp.float32)[:, None]
    leaf_fwd = live * leaf_product(leaf_lower[0], live * leaf_rhs[0])
    leaf_contrib = -leaf_product(leaf_below[0], leaf_fwd)
    own_parent = lax.dynamic_slice_in_dim(leaf_parent, group, 1)
    own_blocks = lax.dynamic_slice(leaf_map, (group, column * leaf_width), (1, leaf_width))
    own_select = leaf_select(own_parent, own_blocks, fronts, column, mid_width)
    column_blocks = lax.dynamic_slice_in_dim(leaf_map, column * leaf_width, leaf_width, 1)
    selection = leaf_select(leaf_parent, column_blocks, fronts, column, mid_width)
    piece = lax.all_gather(leaf_contrib[None], "subtree", axis=0, tiled=True)
    shaped = piece.reshape(piece.shape[0], leaf_width, BLOCK, scenarios)
    assembled = jnp.einsum(
        "phqgk,gkbr->phqbr",
        selection,
        shaped,
        preferred_element_type=jnp.float32,
        precision=lax.Precision.HIGHEST,
    )
    mid_pivot = mid_rhs + assembled[:, 0].reshape(fronts, mid_width * BLOCK, scenarios)
    mid_update = assembled[:, 1].reshape(fronts, mid_width * BLOCK, scenarios)
    mid_fwd = across_front(batched(mid_lower, mid_pivot))
    mid_contrib = mid_update - across_subtree(batched(mid_below, mid_fwd))
    column_map = lax.dynamic_slice_in_dim(mid_map, column * mid_width, mid_width, 1)
    slots = jnp.arange(root_width, dtype=jnp.int32)[:, None, None]
    root_select = (column_map[None, :, :] == column * root_width + slots).astype(jnp.float32)
    root_added = jnp.einsum(
        "qpk,pkbr->qbr",
        root_select,
        mid_contrib.reshape(fronts, mid_width, BLOCK, scenarios),
        preferred_element_type=jnp.float32,
        precision=lax.Precision.HIGHEST,
    )
    root_start = root_rhs + root_added.reshape(root_width * BLOCK, scenarios)
    root_fwd = across_front(
        jnp.dot(
            root_lower,
            root_start,
            preferred_element_type=jnp.float32,
            precision=lax.Precision.HIGHEST,
        )
    )
    root_sol = across_subtree(
        jnp.dot(
            root_upper,
            root_fwd,
            preferred_element_type=jnp.float32,
            precision=lax.Precision.HIGHEST,
        )
    )
    mid_ext = jnp.einsum(
        "qpk,qbr->pkbr",
        root_select,
        root_sol.reshape(root_width, BLOCK, scenarios),
        preferred_element_type=jnp.float32,
        precision=lax.Precision.HIGHEST,
    )
    mid_ext = mid_ext.reshape(fronts, mid_width * BLOCK, scenarios)
    mid_back = mid_fwd - across_front(batched(mid_right, mid_ext))
    mid_sol = across_subtree(batched(mid_upper, mid_back))
    whole_column = jnp.stack(
        [
            mid_sol.reshape(fronts, mid_width, BLOCK, scenarios),
            mid_ext.reshape(fronts, mid_width, BLOCK, scenarios),
        ],
        axis=1,
    )
    leaf_ext = jnp.einsum(
        "phqgk,phqbr->gkbr",
        own_select,
        whole_column,
        preferred_element_type=jnp.float32,
        precision=lax.Precision.HIGHEST,
    )
    leaf_ext = leaf_ext.reshape(local_rows, scenarios)
    leaf_back = live * (leaf_fwd - leaf_product(leaf_right[0], leaf_ext))
    leaf_sol = live * leaf_product(leaf_upper[0], leaf_back)
    return (leaf_sol[None], mid_sol, root_sol)


def solution(mesh):
    return jax.shard_map(
        on_device,
        mesh=mesh,
        in_specs=(
            P("subtree", "front", None),
            P(None, "front", None),
            P("front", None),
            P("subtree", None, "front"),
            P("subtree", None, "front"),
            P("subtree", None, "front"),
            P("subtree", None, "front"),
            P(None, "subtree", "front"),
            P(None, "front", "subtree"),
            P(None, "subtree", "front"),
            P(None, "front", "subtree"),
            P("subtree", "front"),
            P("front", "subtree"),
            P(),
            P(),
            P(),
            P(),
        ),
        out_specs=(P("subtree", "front", None), P(None, "front", None), P("front", None)),
        check_vma=False,
    )
```

profile of v0, /device:TPU:0, one launch (start us, length us, event | category | flops | bytes accessed | tf_op | source)
XLA Modules:
  0.0 725.7 jit_solution(1965828273986753131)
XLA Ops:
  9.1 10.6 %fusion.15 = f32[2048,256]{0,1:T(8,128)} fusion(f32[1,2048,512]{2,1,0:T(8,128)} %param.20, f32[1,512,256]{2,1,0:T(8,128)} %param.17, f32[512]{0:T(512)S(1)} %fusion.57), kind=kOutput, calls=%fused_computation.16 | convolution fusion | flops 3221356544 | bytes 6817792 | tf_op jit(solution)/shard_map/dot_general | solution.py:12
  19.8 38.0 %reduce-scatter.5.cloned.1.call-done = f32[512,256]{0,1:T(8,128)} async-done(((f32[2048,256]{0,1:T(8,128)}), f32[512,256]{0,1:T(8,128)}) %reduce-scatter.5.cloned.1.call-update) | async-done | bytes 524304 | tf_op jit(solution)/shard_map/reduce_scatter | solution.py:11
  57.8 7.3 %fusion.18 = f32[2048,256]{0,1:T(8,128)} fusion(f32[1,2048,512]{2,1,0:T(8,128)} %param.21, f32[512,256]{0,1:T(8,128)} %reduce-scatter.5.cloned.1.call-done, f32[512]{0:T(512)S(1)} %fusion.57), kind=kOutput, calls=%fused_computation.17 | convolution fusion | flops 3221356544 | bytes 6817792 | tf_op jit(solution)/shard_map/dot_general | solution.py:12
  65.2 35.3 %reduce-scatter.7.cloned.1.call-done = f32[512,256]{0,1:T(8,128)} async-done(((f32[2048,256]{0,1:T(8,128)}), f32[512,256]{0,1:T(8,128)}) %reduce-scatter.7.cloned.1.call-update) | async-done | bytes 524304 | tf_op jit(solution)/shard_map/reduce_scatter | solution.py:11
  102.9 46.6 %all-gather.3.cloned.1.call-done = f32[4096,256]{0,1:T(8,128)} async-done(((f32[512,256]{0,1:T(8,128)}), f32[4096,256]{0,1:T(8,128)}) %all-gather.3.cloned.1.call-update) | async-done | bytes 4194320 | tf_op jit(solution)/shard_map/all_gather | solution.py:86
  149.5 6.0 reshape.127
  155.6 6.6 copy.48
  162.2 6.1 convolution_bitcast_fusion.2
  171.2 8.0 %fusion.29 = f32[2,512,256]{1,2,0:T(8,128)} fusion(f32[2,512,1024]{2,1,0:T(8,128)S(1)} %copy-done.2, f32[2,1024,256]{2,1,0:T(8,128)S(1)} %copy-done.6, f32[2,1024,256]{2,1,0:T(8,128)S(1)} %bitcast.122), kind=kOutput, calls=%fused_computation.28 | convolution fusion | flops 3221749760 | bytes 9437184 | tf_op jit(solution)/shard_map/fab,fbr->far/dot_general | solution.py:30
  179.4 51.2 %all-reduce.7.cloned.1.call-done = f32[2,512,256]{1,2,0:T(8,128)} async-done(((f32[2,512,256]{1,2,0:T(8,128)}), f32[2,512,256]{1,2,0:T(8,128)}) %all-reduce.7.cloned.1.call-update) | async-done | bytes 1048592 | tf_op jit(solution)/shard_map/psum | solution.py:22
  230.6 7.5 %convolution_bitcast_fusion.5 = f32[2,1024,256]{1,2,0:T(8,128)} fusion(f32[2,512,256]{1,2,0:T(8,128)} %all-reduce.7.cloned.1.call-done, f32[2,1024,512]{2,1,0:T(8,128)} %param.25), kind=kOutput, calls=%fused_computation.27 | convolution fusion | flops 3221225472 | bytes 7340032 | tf_op jit(solution)/shard_map/fab,fbr->far/dot_general | solution.py:30
  238.3 1.9 copy.33
  242.1 61.3 %all-reduce.9.cloned.1.call-done = f32[2,1024,256]{1,2,0:T(8,128)} async-done(((f32[2,1024,256]{1,2,0:T(8,128)}), f32[2,1024,256]{1,2,0:T(8,128)}) %all-reduce.9.cloned.1.call-update) | async-done | bytes 2097168 | tf_op jit(solution)/shard_map/psum | solution.py:26
  303.4 2.1 sub.9
  305.9 2.0 copy.35
  308.0 3.2 convolution_bitcast_fusion.3
  313.2 26.2 %convolution_bitcast_fusion.1 = f32[1280,256]{0,1:T(8,128)} fusion(f32[2560,256]{1,0:T(8,128)S(1)} %bitcast_add_fusion, f32[1280,2560]{1,0:T(8,128)} %param.28), kind=kOutput, calls=%fused_computation.20 | convolution fusion | flops 10066329600 | bytes 17039360 | tf_op jit(solution)/shard_map/dot_general | solution.py:111
  339.5 56.1 %all-reduce.11.cloned.1.call-done = f32[1280,256]{0,1:T(8,128)} async-done(((f32[1280,256]{0,1:T(8,128)}), f32[1280,256]{0,1:T(8,128)}) %all-reduce.11.cloned.1.call-update) | async-done | bytes 1310736 | tf_op jit(solution)/shard_map/psum | solution.py:22
  395.6 15.6 %convolution_bitcast_fusion = f32[2560,256]{0,1:T(8,128)} fusion(f32[1280,256]{0,1:T(8,128)} %all-reduce.11.cloned.1.call-done, f32[2560,1280]{1,0:T(8,128)} %param.29), kind=kOutput, calls=%fused_computation.12 | convolution fusion | flops 10066329600 | bytes 17039360 | tf_op jit(solution)/shard_map/dot_general | solution.py:119
  411.3 69.2 %all-reduce.13.cloned.1.call-done = f32[2560,256]{0,1:T(8,128)} async-done(((f32[2560,256]{0,1:T(8,128)}), f32[2560,256]{0,1:T(8,128)}) %all-reduce.13.cloned.1.call-update) | async-done | bytes 2621456 | tf_op jit(solution)/shard_map/psum | solution.py:26
  480.5 3.2 copy.37
  483.7 4.4 fusion.12
  490.3 8.0 %convolution_bitcast_fusion.6 = f32[2,512,256]{1,2,0:T(8,128)} fusion(f32[2,1024,256]{2,1,0:T(8,128)S(1)} %bitcast.118, f32[2,512,1024]{2,1,0:T(8,128)S(1)} %copy-done.1), kind=kOutput, calls=%fused_computation.29 | convolution fusion | flops 3221225472 | bytes 7340032 | tf_op jit(solution)/shard_map/fab,fbr->far/dot_general | solution.py:30
  498.6 51.4 %all-reduce.15.cloned.1.call-done = f32[2,512,256]{1,2,0:T(8,128)} async-done(((f32[2,512,256]{1,2,0:T(8,128)}), f32[2,512,256]{1,2,0:T(8,128)}) %all-reduce.15.cloned.1.call-update) | async-done | bytes 1048592 | tf_op jit(solution)/shard_map/psum | solution.py:22
  550.0 7.5 %convolution_bitcast_fusion.4 = f32[2,1024,256]{1,2,0:T(8,128)} fusion(f32[2,1024,512]{2,1,0:T(8,128)} %param.27, f32[2,512,256]{1,2,0:T(8,128)S(1)} %copy-done.4, f32[2,512,256]{1,2,0:T(8,128)} %all-reduce.15.cloned.1.call-done), kind=kOutput, calls=%fused_computation.26 | convolution fusion | flops 3221487616 | bytes 8388608 | tf_op jit(solution)/shard_map/fab,fbr->far/dot_general | solution.py:30
  559.0 63.8 %all-reduce.17.cloned.1.call-done = f32[2,1024,256]{1,2,0:T(8,128)} async-done(((f32[2,1024,256]{1,2,0:T(8,128)}), f32[2,1024,256]{1,2,0:T(8,128)}) %all-reduce.17.cloned.1.call-update) | async-done | bytes 2097168 | tf_op jit(solution)/shard_map/psum | solution.py:26
  622.8 2.9 copy.40
  625.6 2.8 copy.41
  630.6 8.4 %fusion.21 = f32[2048,256]{0,1:T(8,128)} fusion(f32[512,256]{1,0:T(8,128)S(1)} %bitcast.123, f32[1,2048,512]{2,1,0:T(8,128)S(1)} %copy-done.3), kind=kOutput, calls=%fused_computation.18 | convolution fusion | flops 3221225472 | bytes 6815744 | tf_op jit(solution)/shard_map/dot_general | solution.py:12
  639.3 34.6 %reduce-scatter.9.cloned.1.call-done = f32[512,256]{0,1:T(8,128)} async-done(((f32[2048,256]{0,1:T(8,128)}), f32[512,256]{0,1:T(8,128)}) %reduce-scatter.9.cloned.1.call-update) | async-done | bytes 524304 | tf_op jit(solution)/shard_map/reduce_scatter | solution.py:11
  674.0 7.4 %fusion.24 = f32[2048,256]{0,1:T(8,128)} fusion(f32[1,2048,512]{2,1,0:T(8,128)} %param.23, f32[512,256]{0,1:T(8,128)} %reduce-scatter.9.cloned.1.call-done, f32[512,256]{0,1:T(8,128)S(1)} %copy-done.7, f32[512]{0:T(512)S(1)} %fusion.57), kind=kOutput, calls=%fused_computation.19 | convolution fusion | flops 3221618688 | bytes 7342080 | tf_op jit(solution)/shard_map/dot_general | solution.py:12
  681.3 35.3 %reduce-scatter.11.cloned.1.call-done = f32[512,256]{0,1:T(8,128)} async-done(((f32[2048,256]{0,1:T(8,128)}), f32[512,256]{0,1:T(8,128)}) %reduce-scatter.11.cloned.1.call-update) | async-done | bytes 524304 | tf_op jit(solution)/shard_map/reduce_scatter | solution.py:11
  (68 shorter events, 20.8 us)
Async XLA Ops:
  7.2 95.4 %copy-start = (s32[8,16]{1,0:T(8,128)S(1)}, s32[8,16]{1,0:T(8,128)}, u32[]{:S(2)}) copy-start(s32[8,16]{1,0:T(8,128)} %param.32) | copy-start | bytes 1540
  7.2 50.6 %reduce-scatter.5.cloned.1.call-start = ((), (), s32[]{:S(2)}) async-start(), calls=%async_computation.4 | async-start | bytes 2621440 | tf_op jit(solution)/shard_map/reduce_scatter | solution.py:11
  19.7 80.7 %reduce-scatter.7.cloned.1.call-start = ((), (), s32[]{:S(2)}) async-start(), calls=%async_computation.5 | async-start | bytes 2621440 | tf_op jit(solution)/shard_map/reduce_scatter | solution.py:11
  65.1 37.7 %copy-start.9 = (s32[8]{0:T(128)S(1)}, s32[8]{0:T(128)}, u32[]{:S(2)}) copy-start(s32[8]{0:T(128)} %param.30) | copy-start | bytes 100
  65.1 84.4 %all-gather.3.cloned.1.call-start = ((), (), s32[]{:S(2)}) async-start(), calls=%async_computation.14 | async-start | bytes 4718592 | tf_op jit(solution)/shard_map/all_gather | solution.py:86
  102.4 128.2 %all-reduce.7.cloned.1.call-start = ((), (), s32[]{:S(2)}) async-start(), calls=%async_computation.6 | async-start | bytes 2097152 | tf_op jit(solution)/shard_map/psum | solution.py:22
  168.3 1.6 copy-start.6
  168.6 2.5 copy-start.2
  179.2 59.0 %copy-start.8 = (s32[2,32]{1,0:T(2,128)S(1)}, s32[2,32]{1,0:T(2,128)}, u32[]{:S(2)}) copy-start(s32[2,32]{1,0:T(2,128)} %param.33) | copy-start | bytes 772
  179.2 124.2 %all-reduce.9.cloned.1.call-start = ((), (), s32[]{:S(2)}) async-start(), calls=%async_computation.7 | async-start | bytes 4194304 | tf_op jit(solution)/shard_map/psum | solution.py:26
  238.1 157.4 %all-reduce.11.cloned.1.call-start = ((), (), s32[]{:S(2)}) async-start(), calls=%async_computation.8 | async-start | bytes 2621440 | tf_op jit(solution)/shard_map/psum | solution.py:22
  311.2 1.7 copy-start.5
  339.4 141.1 %all-reduce.13.cloned.1.call-start = ((), (), s32[]{:S(2)}) async-start(), calls=%async_computation.9 | async-start | bytes 5242880 | tf_op jit(solution)/shard_map/psum | solution.py:26
  411.2 138.8 %all-reduce.15.cloned.1.call-start = ((), (), s32[]{:S(2)}) async-start(), calls=%async_computation.10 | async-start | bytes 2097152 | tf_op jit(solution)/shard_map/psum | solution.py:22
  488.1 2.2 copy-start.1
  490.3 59.8 %copy-start.4 = (f32[2,512,256]{1,2,0:T(8,128)S(1)}, f32[2,512,256]{1,2,0:T(8,128)}, u32[]{:S(2)}) copy-start(f32[2,512,256]{1,2,0:T(8,128)} %all-reduce.7.cloned.1.call-done) | copy-start | bytes 3145732
  498.3 124.4 %all-reduce.17.cloned.1.call-start = ((), (), s32[]{:S(2)}) async-start(), calls=%async_computation.11 | async-start | bytes 4194304 | tf_op jit(solution)/shard_map/psum | solution.py:26
  557.5 116.4 %reduce-scatter.9.cloned.1.call-start = ((), (), s32[]{:S(2)}) async-start(), calls=%async_computation.12 | async-start | bytes 2621440 | tf_op jit(solution)/shard_map/reduce_scatter | solution.py:11
  628.5 2.2 copy-start.3
  630.6 43.3 %copy-start.7 = (f32[512,256]{0,1:T(8,128)S(1)}, f32[512,256]{0,1:T(8,128)}, u32[]{:S(2)}) copy-start(f32[512,256]{0,1:T(8,128)} %reduce-scatter.5.cloned.1.call-done) | copy-start | bytes 1572868
  639.0 77.7 %reduce-scatter.11.cloned.1.call-start = ((), (), s32[]{:S(2)}) async-start(), calls=%async_computation.13 | async-start | bytes 2621440 | tf_op jit(solution)/shard_map/reduce_scatter | solution.py:11
Sparse Core Ops, SparseCore 0:
  19.8 37.9 reduce-scatter.4
  65.2 35.1 reduce-scatter.6
  102.6 46.8 all-gather.2
  179.3 51.2 all-reduce.6
  238.2 65.1 all-reduce.8
  339.6 55.9 all-reduce.10
  411.3 69.0 all-reduce.12
  498.4 51.5 all-reduce.14
  557.6 65.0 all-reduce.16
  639.1 34.7 reduce-scatter.8
  681.5 35.1 reduce-scatter.10
where the time goes:
time: 734 us; the launch traced here: 726 us
  waiting for transfers between devices  543 us (74%)
  matrix products  122 us (17%)
  local copies, waits for them, and re-layouts  38.1 us (5%)
  between operations  14.5 us (2%)
    psum x3, waiting for transfers between devices, across_subtree(): return lax.psum(partial_value, 'subtree')  194 us
    psum x3, waiting for transfers between devices, across_front(): return lax.psum(partial_value, 'front')  159 us
    reduce_scatter x4, waiting for transfers between devices, leaf_product(): lax.psum_scatter(jnp.dot(matrix, vector, preferred_element_type=jnp.float...  143 us
    all_gather x1, waiting for transfers between devices, on_device(): piece = lax.all_gather(leaf_contrib[None], 'subtree', axis=0, tiled=True)  46.6 us
    dot_general x4, matrix products, leaf_product(): jnp.dot(matrix, vector, preferred_element_type=jnp.float32, precision=lax...  33.6 us
    dot_general x4, matrix products, batched(): jnp.einsum('fab,fbr->far', matrix, vector, preferred_element_type=jnp.flo...  31 us
    dot_general x1, matrix products, on_device(): jnp.dot(root_lower, root_start, preferred_element_type=jnp.float32, preci...  26.2 us
    dot_general x1, matrix products, on_device(): jnp.dot(root_upper, root_fwd, preferred_element_type=jnp.float32, precisi...  15.6 us
  transfers between devices with their start and end apart: 11, of which 11 were waited for; matrix products, arithmetic and copies ran while one was open for 1% of the time, Pallas kernels for 0%

commit v1 on v0

--- a/solution.py
+++ b/solution.py
@@ -23,7 +23,7 @@
 
 
 def across_subtree(partial_value):
-    return lax.psum(partial_value, "subtree")
+    return jnp.sum(lax.all_gather(partial_value, "subtree"), axis=0)
 
 
 def batched(matrix, vector):

time: 734 us -> 1060 us (1.44)
  waiting for transfers between devices: 543 us -> 832 us
  other arithmetic: 6.88 us -> 27.6 us
  local copies, waits for them, and re-layouts: 38.1 us -> 57.4 us
    all_gather x0 -> x3, waiting for transfers between devices: none -> 486 us  [across_subtree(): return jnp.sum(lax.all_gather(partial_value, 'subtree'), axis=0)]
    psum x3 -> x0, waiting for transfers between devices: 194 us -> none  [across_subtree(): return lax.psum(partial_value, 'subtree')]
    unnamed x22 -> x24, local copies, waits for them, and re-layouts: 5.98 us -> 30.5 us
    reduce_sum x0 -> x3, other arithmetic: none -> 22.8 us  [across_subtree(): return jnp.sum(lax.all_gather(partial_value, 'subtree'), axis=0)]
  transfers between devices with their start and end apart: 11 -> 11, of which waited for: 11 -> 11; matrix products, arithmetic and copies ran while one was open for 1% -> 0% of each run, Pallas kernels for 0% -> 0%
where the time goes in v1:
time: 1060 us; the launch traced here: 1050 us
  waiting for transfers between devices  832 us (78%)
  matrix products  122 us (12%)
  local copies, waits for them, and re-layouts  57.4 us (5%)
  other arithmetic  27.6 us (3%)
  between operations  14.5 us (1%)
    all_gather x3, waiting for transfers between devices, across_subtree(): return jnp.sum(lax.all_gather(partial_value, 'subtree'), axis=0)  486 us
    psum x3, waiting for transfers between devices, across_front(): return lax.psum(partial_value, 'front')  157 us
    reduce_scatter x4, waiting for transfers between devices, leaf_product(): lax.psum_scatter(jnp.dot(matrix, vector, preferred_element_type=jnp.float...  142 us
    all_gather x1, waiting for transfers between devices, on_device(): piece = lax.all_gather(leaf_contrib[None], 'subtree', axis=0, tiled=True)  46.6 us
    dot_general x4, matrix products, leaf_product(): jnp.dot(matrix, vector, preferred_element_type=jnp.float32, precision=lax...  33.6 us
    unnamed x24, local copies, waits for them, and re-layouts  30.5 us
    dot_general x4, matrix products, batched(): jnp.einsum('fab,fbr->far', matrix, vector, preferred_element_type=jnp.flo...  29.9 us
    dot_general x1, matrix products, on_device(): jnp.dot(root_lower, root_start, preferred_element_type=jnp.float32, preci...  25.9 us
  transfers between devices with their start and end apart: 11, of which 11 were waited for; matrix products, arithmetic and copies ran while one was open for 0% of the time, Pallas kernels for 0%

profile of v1, /device:TPU:0, one launch (start us, length us, event | category | flops | bytes accessed | tf_op | source)
XLA Modules:
  0.0 1054.3 jit_solution(7817309470348441923)
XLA Ops:
  9.1 10.5 fusion.15
  19.7 38.0 %reduce-scatter.5.cloned.1.call-done = f32[512,256]{0,1:T(8,128)} async-done(((f32[2048,256]{0,1:T(8,128)}), f32[512,256]{0,1:T(8,128)}) %reduce-scatter.5.cloned.1.call-update) | async-done | bytes 524304 | tf_op jit(solution)/shard_map/reduce_scatter | solution.py:11
  57.8 7.3 fusion.18
  65.2 35.3 %reduce-scatter.7.cloned.1.call-done = f32[512,256]{0,1:T(8,128)} async-done(((f32[2048,256]{0,1:T(8,128)}), f32[512,256]{0,1:T(8,128)}) %reduce-scatter.7.cloned.1.call-update) | async-done | bytes 524304 | tf_op jit(solution)/shard_map/reduce_scatter | solution.py:11
  102.9 46.6 %all-gather.9.cloned.1.call-done = f32[4096,256]{0,1:T(8,128)} async-done(((f32[512,256]{0,1:T(8,128)}), f32[4096,256]{0,1:T(8,128)}) %all-gather.9.cloned.1.call-update) | async-done | bytes 4194320 | tf_op jit(solution)/shard_map/all_gather | solution.py:86
  149.5 6.0 reshape.127
  155.5 6.6 copy.86
  162.1 6.0 convolution_bitcast_fusion.2
  172.5 7.8 fusion.36
  180.4 51.4 %all-reduce.4.cloned.1.call-done = f32[2,512,256]{1,2,0:T(8,128)} async-done(((f32[2,512,256]{1,2,0:T(8,128)}), f32[2,512,256]{1,2,0:T(8,128)}) %all-reduce.4.cloned.1.call-update) | async-done | bytes 1048592 | tf_op jit(solution)/shard_map/psum | solution.py:22
  231.8 6.6 convolution_bitcast_fusion.4
  240.4 151.1 %all-gather.11.cloned.1.call-done = f32[16,1024,256]{2,1,0:T(8,128)} async-done(((f32[2,1024,256]{2,1,0:T(8,128)}), f32[16,1024,256]{2,1,0:T(8,128)}) %all-gather.11.cloned.1.call-update) | async-done | bytes 16777232 | tf_op jit(solution)/shard_map/all_gather | solution.py:26
  391.5 7.3 reduce_sum.29
  398.7 4.3 fusion.33
  405.1 25.9 %convolution_bitcast_fusion.1 = f32[1280,256]{0,1:T(8,128)} fusion(f32[2560,256]{1,0:T(8,128)S(1)} %bitcast_add_fusion, f32[1280,2560]{1,0:T(8,128)} %param.28), kind=kOutput, calls=%fused_computation.21 | convolution fusion | flops 10066329600 | bytes 17039360 | tf_op jit(solution)/shard_map/dot_general | solution.py:111
  431.1 54.7 %all-reduce.6.cloned.1.call-done = f32[1280,256]{0,1:T(8,128)} async-done(((f32[1280,256]{0,1:T(8,128)}), f32[1280,256]{0,1:T(8,128)}) %all-reduce.6.cloned.1.call-update) | async-done | bytes 1310736 | tf_op jit(solution)/shard_map/psum | solution.py:22
  485.8 15.9 %convolution_bitcast_fusion = f32[2560,256]{0,1:T(8,128)} fusion(f32[1280,256]{0,1:T(8,128)} %all-reduce.6.cloned.1.call-done, f32[2560,1280]{1,0:T(8,128)} %param.29), kind=kOutput, calls=%fused_computation.13 | convolution fusion | flops 10066329600 | bytes 17039360 | tf_op jit(solution)/shard_map/dot_general | solution.py:119
  501.8 185.6 %all-gather.13.cloned.1.call-done = f32[20480,256]{0,1:T(8,128)} async-done(((f32[2560,256]{0,1:T(8,128)}), f32[20480,256]{0,1:T(8,128)}) %all-gather.13.cloned.1.call-update) | async-done | bytes 20971536 | tf_op jit(solution)/shard_map/all_gather | solution.py:26
  687.3 23.4 %copy.98 = f32[32,8,8,2560]{3,2,1,0:T(8,128)S(1)} copy(f32[32,8,8,2560]{3,1,2,0:T(8,128)} %bitcast.125) | data formatting | bytes 41943040
  710.7 7.1 bitcast_reduce_fusion
  720.1 4.4 fusion.12
  726.6 8.0 convolution_bitcast_fusion.5
  734.7 50.8 %all-reduce.8.cloned.1.call-done = f32[2,512,256]{1,2,0:T(8,128)} async-done(((f32[2,512,256]{1,2,0:T(8,128)}), f32[2,512,256]{1,2,0:T(8,128)}) %all-reduce.8.cloned.1.call-update) | async-done | bytes 1048592 | tf_op jit(solution)/shard_map/psum | solution.py:22
  785.5 7.5 convolution_bitcast_fusion.3
  793.0 2.9 copy.76
  797.6 149.6 %all-gather.15.cloned.1.call-done = f32[16,1024,256]{2,1,0:T(8,128)} async-done(((f32[2,1024,256]{2,1,0:T(8,128)}), f32[16,1024,256]{2,1,0:T(8,128)}) %all-gather.15.cloned.1.call-update) | async-done | bytes 16777232 | tf_op jit(solution)/shard_map/all_gather | solution.py:26
  947.1 8.5 reduce_sum.32
  955.6 2.8 copy.79
  960.6 8.4 fusion.21
  969.3 33.2 %reduce-scatter.9.cloned.1.call-done = f32[512,256]{0,1:T(8,128)} async-done(((f32[2048,256]{0,1:T(8,128)}), f32[512,256]{0,1:T(8,128)}) %reduce-scatter.9.cloned.1.call-update) | async-done | bytes 524304 | tf_op jit(solution)/shard_map/reduce_scatter | solution.py:11
  1002.5 7.4 fusion.24
  1009.9 35.4 %reduce-scatter.11.cloned.1.call-done = f32[512,256]{0,1:T(8,128)} async-done(((f32[2048,256]{0,1:T(8,128)}), f32[512,256]{0,1:T(8,128)}) %reduce-scatter.11.cloned.1.call-update) | async-done | bytes 524304 | tf_op jit(solution)/shard_map/reduce_scatter | solution.py:11
  (70 shorter events, 23.7 us)
Async XLA Ops:
  7.2 95.4 %copy-start = (s32[8,16]{1,0:T(8,128)S(1)}, s32[8,16]{1,0:T(8,128)}, u32[]{:S(2)}) copy-start(s32[8,16]{1,0:T(8,128)} %param.32) | copy-start | bytes 1540
  7.2 50.6 %reduce-scatter.5.cloned.1.call-start = ((), (), s32[]{:S(2)}) async-start(), calls=%async_computation.4 | async-start | bytes 2621440 | tf_op jit(solution)/shard_map/reduce_scatter | solution.py:11
  19.7 80.7 %reduce-scatter.7.cloned.1.call-start = ((), (), s32[]{:S(2)}) async-start(), calls=%async_computation.5 | async-start | bytes 2621440 | tf_op jit(solution)/shard_map/reduce_scatter | solution.py:11
  65.1 37.7 %copy-start.10 = (s32[8]{0:T(128)S(1)}, s32[8]{0:T(128)}, u32[]{:S(2)}) copy-start(s32[8]{0:T(128)} %param.30) | copy-start | bytes 100
  65.1 84.4 %all-gather.9.cloned.1.call-start = ((), (), s32[]{:S(2)}) async-start(), calls=%async_computation.11 | async-start | bytes 4718592 | tf_op jit(solution)/shard_map/all_gather | solution.py:86
  102.3 129.5 %all-reduce.4.cloned.1.call-start = ((), (), s32[]{:S(2)}) async-start(), calls=%async_computation.6 | async-start | bytes 2097152 | tf_op jit(solution)/shard_map/psum | solution.py:22
  168.2 2.1 copy-start.1
  168.2 3.1 copy-start.7
  168.3 4.2 copy-start.3
  180.4 211.1 %all-gather.11.cloned.1.call-start = ((), (), s32[]{:S(2)}) async-start(), calls=%async_computation.12 | async-start | bytes 18874368 | tf_op jit(solution)/shard_map/all_gather | solution.py:26
  238.4 1.9 copy-start.9
  240.2 245.6 %all-reduce.6.cloned.1.call-start = ((), (), s32[]{:S(2)}) async-start(), calls=%async_computation.7 | async-start | bytes 2621440 | tf_op jit(solution)/shard_map/psum | solution.py:22
  403.1 1.7 copy-start.6
  431.1 256.2 %all-gather.13.cloned.1.call-start = ((), (), s32[]{:S(2)}) async-start(), calls=%async_computation.13 | async-start | bytes 23592960 | tf_op jit(solution)/shard_map/all_gather | solution.py:26
  501.7 283.8 %all-reduce.8.cloned.1.call-start = ((), (), s32[]{:S(2)}) async-start(), calls=%async_computation.8 | async-start | bytes 2097152 | tf_op jit(solution)/shard_map/psum | solution.py:22
  724.4 2.2 copy-start.2
  726.6 58.9 %copy-start.5 = (f32[2,512,256]{1,2,0:T(8,128)S(1)}, f32[2,512,256]{1,2,0:T(8,128)}, u32[]{:S(2)}) copy-start(f32[2,512,256]{1,2,0:T(8,128)} %all-reduce.4.cloned.1.call-done) | copy-start | bytes 3145732
  734.7 212.4 %all-gather.15.cloned.1.call-start = ((), (), s32[]{:S(2)}) async-start(), calls=%async_computation.14 | async-start | bytes 18874368 | tf_op jit(solution)/shard_map/all_gather | solution.py:26
  795.9 206.6 %reduce-scatter.9.cloned.1.call-start = ((), (), s32[]{:S(2)}) async-start(), calls=%async_computation.9 | async-start | bytes 2621440 | tf_op jit(solution)/shard_map/reduce_scatter | solution.py:11
  958.4 2.2 copy-start.4
  960.6 41.9 %copy-start.8 = (f32[512,256]{0,1:T(8,128)S(1)}, f32[512,256]{0,1:T(8,128)}, u32[]{:S(2)}) copy-start(f32[512,256]{0,1:T(8,128)} %reduce-scatter.5.cloned.1.call-done) | copy-start | bytes 1572868
  969.0 76.3 %reduce-scatter.11.cloned.1.call-start = ((), (), s32[]{:S(2)}) async-start(), calls=%async_computation.10 | async-start | bytes 2621440 | tf_op jit(solution)/shard_map/reduce_scatter | solution.py:11
Sparse Core Ops, SparseCore 0:
  19.8 37.9 reduce-scatter.4
  65.2 35.1 reduce-scatter.6
  102.6 46.8 all-gather.8
  180.5 51.2 all-reduce.3
  240.4 151.0 all-gather.10
  431.2 54.5 all-reduce.5
  501.8 185.4 all-gather.12
  734.8 50.6 all-reduce.7
  796.0 151.0 all-gather.14
  969.1 33.3 reduce-scatter.8
  1010.0 35.1 reduce-scatter.10
